TPU v7x, 32 devices: a whole 2x2x4 slice. The times are simulated.
32 devices in a mesh: dp: 16 (over z, y, x), mp: 2 (over core).
Axes of the slice: x: 2, y: 2, z: 4, core: 2. Of those that a mesh axis runs over, the one named last changes fastest.
Arguments:
- pixels: bfloat16 [16, 13, 256, 256], P('dp'), may hold values from -6 to 6
- band_count: int32 [16], P('dp'), may hold values from 1 to 13
- wavelengths: int32 [16, 13], P('dp'), may hold values from 40 to 249
- size_class: int32 [16], P('dp'), may hold values from 0 to 2
- token_keep: int32 [16, 256], P('dp'), may hold values 0 or 1
- hyp_attn: float32 [4, 128, 128], replicated, may hold values from -0.75 to 0.75
- hyp_mlp_in: float32 [128, 2048], replicated, may hold values from -0.5 to 0.5
- hyp_mlp_out: float32 [2048, 128], replicated, may hold values from -0.125 to 0.125
- hyp_gain: float32 [2, 128], replicated, may hold values from 0.5 to 1.5
- hyp_shift: float32 [2, 128], replicated, may hold values from -4 to 4
- bias_token: float32 [128], replicated, may hold values from -6 to 6
- kern_weight: float32 [128, 768, 256], P(None, 'dp'), may hold values from -0.009765625 to 0.009765625
- kern_bias: float32 [768, 256], P('dp'), may hold values from -0.125 to 0.125
- patch_bias_weight: float32 [128, 768], replicated, may hold values from -0.5 to 0.5
- norm_gain: float32 [2, 768], replicated, may hold values from 0.5 to 1.5
- norm_shift: float32 [2, 768], replicated, may hold values from -4 to 4
- attn_in: float32 [3, 768, 768], P(None, 'dp', 'mp'), may hold values from -0.21875 to 0.21875
- attn_in_bias: float32 [2, 768], P(None, 'mp'), may hold values from -4 to 4
- attn_out: float32 [768, 768], P('dp', 'mp'), may hold values from -0.625 to 0.625
- attn_out_bias: float32 [768], replicated, may hold values from -4 to 4
- mlp_in: float32 [768, 3072], P('dp', 'mp'), may hold values from -0.21875 to 0.21875
- mlp_in_bias: float32 [3072], P('mp'), may hold values from -4 to 4
- mlp_out: float32 [768, 3072], P('dp', 'mp'), may hold values from -0.109375 to 0.109375
- mlp_out_bias: float32 [768], replicated, may hold values from -4 to 4
- cotangent: bfloat16 [16, 256, 768], P('dp'), may hold values from -6 to 6
Outputs:
- layer_out: bfloat16 [16, 256, 768], P('dp')
- pixel_grad: bfloat16 [16, 13, 256, 256], P('dp')
- grad_hyp_attn: float32 [4, 128, 128], replicated
- grad_hyp_mlp_in: float32 [128, 2048], replicated
- grad_hyp_mlp_out: float32 [2048, 128], replicated
- grad_hyp_gain: float32 [2, 128], replicated
- grad_hyp_shift: float32 [2, 128], replicated
- grad_bias_token: float32 [128], replicated
- grad_kern_weight: float32 [128, 768, 256], P(None, 'dp')
- grad_kern_bias: float32 [768, 256], P('dp')
- grad_patch_bias_weight: float32 [128, 768], replicated
- grad_norm_gain: float32 [2, 768], replicated
- grad_norm_shift: float32 [2, 768], replicated
- grad_attn_in: float32 [3, 768, 768], P(None, 'dp', 'mp')
- grad_attn_in_bias: float32 [2, 768], P(None, 'mp')
- grad_attn_out: float32 [768, 768], P('dp', 'mp')
- grad_attn_out_bias: float32 [768], replicated
- grad_mlp_in: float32 [768, 3072], P('dp', 'mp')
- grad_mlp_in_bias: float32 [3072], P('mp')
- grad_mlp_out: float32 [768, 3072], P('dp', 'mp')
- grad_mlp_out_bias: float32 [768], replicated
Inputs may be any that keep to these rules, and one draw needn't show every extreme that they name: Bands 0 to band_count[s] - 1 of slot s are present.
All inputs are finite; a program needn't handle non-finite values. No bound on the sum of `token_keep` on one device may be relied on, other than what follows from the above.
Results may differ from a plain program's by a relative error of at most 0.013.
Values may be sent and summed in bfloat16 or wider, within the bound.
A program may use at most 192 MiB of HBM per device.

v0:
```python
from functools import partial
import math
import jax
import jax.numpy as jnp
from jax import lax
from jax.sharding import PartitionSpec as P

HEAD_DIM = 64
HYP_HEADS = 4
vit_epsilon = 1e-06
hyper_epsilon = 1e-05


def exact_einsum(pattern, left_side, right_side):
    return jnp.einsum(
        pattern,
        left_side,
        right_side,
        precision=lax.Precision.HIGHEST,
        preferred_element_type=jnp.float32,
    )


def fast_einsum(pattern, left_side, right_side):
    return jnp.einsum(pattern, left_side, right_side, preferred_element_type=jnp.float32)


def norm_rows(values, gain_row, shift_row, epsilon):
    center = values - jnp.mean(values, axis=-1, keepdims=True)
    spread = jnp.mean(center * center, axis=-1, keepdims=True)
    return center * lax.rsqrt(spread + epsilon) * gain_row + shift_row


def exact_gelu(values):
    return jax.nn.gelu(values, approximate=False)


def wave_embedding(wavelengths, model_width):
    half_width = model_width // 2
    frequency = 10000.0 ** (-jnp.arange(half_width, dtype=jnp.float32) * 2.0 / model_width)
    angles = wavelengths.astype(jnp.float32)[..., None] * frequency
    return jnp.concatenate([jnp.sin(angles), jnp.cos(angles)], axis=-1)


def hyper_slot(
    embedding, band_valid, hyp_attn, hyp_mlp_in, hyp_mlp_out, hyp_gain, hyp_shift, bias_token
):
    model_width = embedding.shape[-1]
    sequence = jnp.concatenate([embedding, bias_token[None, :]], axis=0)
    keys_valid = jnp.concatenate([band_valid, jnp.ones((1,), dtype=bool)])
    length = sequence.shape[0]
    head_size = model_width // HYP_HEADS
    query_rows = exact_einsum("te,ef->tf", sequence, hyp_attn[0]).reshape(
        length, HYP_HEADS, head_size
    )
    key_rows = exact_einsum("te,ef->tf", sequence, hyp_attn[1]).reshape(
        length, HYP_HEADS, head_size
    )
    value_rows = exact_einsum("te,ef->tf", sequence, hyp_attn[2]).reshape(
        length, HYP_HEADS, head_size
    )
    scores = exact_einsum("qhd,khd->hqk", query_rows, key_rows) * (1.0 / math.sqrt(head_size))
    scores = jnp.where(keys_valid[None, None, :], scores, -1e30)
    weights = jax.nn.softmax(scores, axis=-1)
    mixed_rows = exact_einsum("hqk,khd->qhd", weights, value_rows).reshape(length, model_width)
    first_rows = norm_rows(
        sequence + exact_einsum("te,ef->tf", mixed_rows, hyp_attn[3]),
        hyp_gain[0],
        hyp_shift[0],
        hyper_epsilon,
    )
    inner_rows = exact_gelu(exact_einsum("te,ef->tf", first_rows, hyp_mlp_in))
    second_rows = norm_rows(
        first_rows + exact_einsum("tf,fe->te", inner_rows, hyp_mlp_out),
        hyp_gain[1],
        hyp_shift[1],
        hyper_epsilon,
    )
    return (second_rows[:-1] + embedding, second_rows[-1])


def hyper_all(
    embed_rows, valid_rows, attn_w, mlp_first, mlp_second, gain_rows, shift_rows, token_row, bias_w
):
    code_vals, tail_rows = jax.vmap(hyper_slot, in_axes=(0, 0, None, None, None, None, None, None))(
        embed_rows, valid_rows, attn_w, mlp_first, mlp_second, gain_rows, shift_rows, token_row
    )
    return (code_vals, exact_einsum("se,ec->sc", tail_rows, bias_w))


def per_device(
    pixels,
    band_count,
    wavelengths,
    size_class,
    token_keep,
    hyp_attn,
    hyp_mlp_in,
    hyp_mlp_out,
    hyp_gain,
    hyp_shift,
    bias_token,
    kern_weight,
    kern_bias,
    patch_bias_weight,
    norm_gain,
    norm_shift,
    attn_in,
    attn_in_bias,
    attn_out,
    attn_out_bias,
    mlp_in,
    mlp_in_bias,
    mlp_out,
    mlp_out_bias,
    cotangent,
):
    slot_count, band_total, row_total, pix_size = pixels.shape
    model_width = norm_gain.shape[1]
    hyper_width = hyp_attn.shape[1]
    tokens = slot_count * row_total
    embedding = wave_embedding(wavelengths, hyper_width)
    band_valid = jnp.arange(band_total)[None, :] < band_count[:, None]
    live_rows = jnp.where(
        size_class == 0,
        row_total * 49 // 256,
        jnp.where(size_class == 1, row_total * 196 // 256, row_total),
    )
    position = jnp.arange(row_total)
    row_valid = position[None, :] < live_rows[:, None]
    key_valid = row_valid & ((token_keep == 1) | (position[None, :] == 0))
    row_scale = row_valid.astype(jnp.float32).reshape(tokens, 1)
    band_mask = band_valid.astype(jnp.bfloat16)[:, :, None, None]
    hyper_local = partial(hyper_all, embedding, band_valid)
    (code_vals, patch_bias), hyper_back = jax.vjp(
        hyper_local,
        hyp_attn,
        hyp_mlp_in,
        hyp_mlp_out,
        hyp_gain,
        hyp_shift,
        bias_token,
        patch_bias_weight,
    )
    code_rows = code_vals.astype(jnp.bfloat16).reshape(slot_count * band_total, hyper_width)
    all_codes = lax.all_gather(code_rows, "dp", axis=0, tiled=True)
    kern_low = kern_weight.astype(jnp.bfloat16)
    local_full = (fast_einsum("ne,ecp->ncp", all_codes, kern_low) + kern_bias).astype(jnp.bfloat16)
    kernel = lax.all_to_all(local_full, "dp", split_axis=0, concat_axis=1, tiled=True)
    kernel = kernel.reshape(slot_count, band_total, model_width, pix_size)
    masked_pixels = pixels * band_mask
    embedded = fast_einsum("sbtp,sbcp->stc", masked_pixels, kernel) + patch_bias[:, None, :]
    embedded = embedded.reshape(tokens, model_width)
    weight_shards = (
        attn_in.astype(jnp.bfloat16),
        attn_out.astype(jnp.bfloat16),
        mlp_in.astype(jnp.bfloat16),
        mlp_out.astype(jnp.bfloat16),
    )
    gathered_in, gathered_out, gathered_up, gathered_down = (
        lax.all_gather(weight_shards[0], "dp", axis=1, tiled=True),
        lax.all_gather(weight_shards[1], "dp", axis=0, tiled=True),
        lax.all_gather(weight_shards[2], "dp", axis=0, tiled=True),
        lax.all_gather(weight_shards[3], "dp", axis=0, tiled=True),
    )
    local_heads = gathered_in.shape[2] // HEAD_DIM
    head_grid = (slot_count, row_total, local_heads, HEAD_DIM)
    score_scale = 1.0 / math.sqrt(HEAD_DIM)
    key_open = key_valid[:, None, None, :]
    norm_one = partial(norm_rows, epsilon=vit_epsilon)
    normed_a, first_back = jax.vjp(norm_one, embedded, norm_gain[0], norm_shift[0])
    normed_a = normed_a.astype(jnp.bfloat16)
    input_bias = jnp.stack([attn_in_bias[0], jnp.zeros_like(attn_in_bias[0]), attn_in_bias[1]])[
        :, None, :
    ]
    projected = (fast_einsum("nd,jde->jne", normed_a, gathered_in) + input_bias).astype(
        jnp.bfloat16
    )
    query_rows = projected[0].reshape(head_grid)
    key_rows = projected[1].reshape(head_grid)
    value_rows = projected[2].reshape(head_grid)
    scores = jnp.where(
        key_open, fast_einsum("sqhd,skhd->shqk", query_rows, key_rows) * score_scale, -1e30
    )
    row_peak = jnp.max(scores, axis=-1, keepdims=True)
    exp_scores = jnp.exp(scores - row_peak)
    prob_total = jnp.sum(exp_scores, axis=-1, keepdims=True)
    log_total = row_peak + jnp.log(prob_total)
    prob_low = (exp_scores / prob_total).astype(jnp.bfloat16)
    context = (
        fast_einsum("shqk,skhd->sqhd", prob_low, value_rows)
        .reshape(tokens, local_heads * HEAD_DIM)
        .astype(jnp.bfloat16)
    )
    head_part = fast_einsum("ne,de->nd", context, gathered_out)
    middle = embedded + lax.psum(head_part, "mp") + attn_out_bias
    normed_b, second_back = jax.vjp(norm_one, middle, norm_gain[1], norm_shift[1])
    normed_b = normed_b.astype(jnp.bfloat16)
    pre_act = fast_einsum("nd,df->nf", normed_b, gathered_up) + mlp_in_bias
    activation, gelu_back = jax.vjp(exact_gelu, pre_act)
    activation = activation.astype(jnp.bfloat16)
    unit_part = fast_einsum("nf,df->nd", activation, gathered_down)
    final_rows = (
        middle + lax.psum(unit_part.astype(jnp.bfloat16), "mp").astype(jnp.float32) + mlp_out_bias
    ) * row_scale
    layer_out = final_rows.astype(jnp.bfloat16).reshape(slot_count, row_total, model_width)
    gathered_in, gathered_out, gathered_up, gathered_down = (
        lax.all_gather(weight_shards[0], "dp", axis=1, tiled=True),
        lax.all_gather(weight_shards[1], "dp", axis=0, tiled=True),
        lax.all_gather(weight_shards[2], "dp", axis=0, tiled=True),
        lax.all_gather(weight_shards[3], "dp", axis=0, tiled=True),
    )
    out_grad = cotangent.reshape(tokens, model_width).astype(jnp.float32) * row_scale
    out_grad_low = out_grad.astype(jnp.bfloat16)
    grad_mlp_out_bias = jnp.sum(out_grad, axis=0)
    grad_down = fast_einsum("nd,nf->df", out_grad_low, activation)
    act_grad = fast_einsum("nd,df->nf", out_grad_low, gathered_down).astype(jnp.bfloat16)
    pre_grad = gelu_back(act_grad.astype(jnp.float32))[0].astype(jnp.bfloat16)
    grad_mlp_in_bias = jnp.sum(pre_grad, axis=0, dtype=jnp.float32)
    grad_up = fast_einsum("nd,nf->df", normed_b, pre_grad)
    second_part = fast_einsum("nf,df->nd", pre_grad, gathered_up)
    middle_in, gain_second, shift_second = second_back(lax.psum(second_part, "mp"))
    middle_grad = out_grad + middle_in
    attended_grad = middle_grad.astype(jnp.bfloat16)
    grad_attn_out_bias = jnp.sum(attended_grad, axis=0, dtype=jnp.float32)
    grad_proj = fast_einsum("nd,ne->de", attended_grad, context)
    context_grad = (
        fast_einsum("nd,de->ne", attended_grad, gathered_out)
        .astype(jnp.bfloat16)
        .reshape(head_grid)
    )
    scores_again = jnp.where(
        key_open, fast_einsum("sqhd,skhd->shqk", query_rows, key_rows) * score_scale, -1e30
    )
    prob_full = jnp.exp(scores_again - log_total)
    prob_grad = fast_einsum("sqhd,skhd->shqk", context_grad, value_rows)
    row_inner = jnp.sum(prob_full * prob_grad, axis=-1, keepdims=True)
    score_grad = (prob_full * (prob_grad - row_inner)).astype(jnp.bfloat16)
    query_grad = fast_einsum("shqk,skhd->sqhd", score_grad, key_rows) * score_scale
    key_grad = fast_einsum("shqk,sqhd->skhd", score_grad, query_rows) * score_scale
    value_grad = fast_einsum("shqk,sqhd->skhd", prob_low, context_grad)
    qkv_grad = (
        jnp.stack([query_grad, key_grad, value_grad])
        .reshape(3, tokens, local_heads * HEAD_DIM)
        .astype(jnp.bfloat16)
    )
    grad_in_bias = jnp.stack(
        [
            jnp.sum(qkv_grad[0], axis=0, dtype=jnp.float32),
            jnp.sum(qkv_grad[2], axis=0, dtype=jnp.float32),
        ]
    )
    grad_in = fast_einsum("nd,jne->jde", normed_a, qkv_grad)
    first_part = fast_einsum("jne,jde->nd", qkv_grad, gathered_in)
    embed_in, gain_first, shift_first = first_back(lax.psum(first_part, "mp"))
    embed_grad = (
        (middle_grad + embed_in).astype(jnp.bfloat16).reshape(slot_count, row_total, model_width)
    )
    patch_bias_grad = jnp.sum(embed_grad, axis=1, dtype=jnp.float32)
    band_float = band_valid.astype(jnp.float32)[:, :, None, None]
    pixel_grad = (fast_einsum("stc,sbcp->sbtp", embed_grad, kernel) * band_float).astype(
        jnp.bfloat16
    )
    kernel_grad = (
        fast_einsum("stc,sbtp->sbcp", embed_grad, masked_pixels)
        .astype(jnp.bfloat16)
        .reshape(slot_count * band_total, model_width, pix_size)
    )
    local_grad = lax.all_to_all(kernel_grad, "dp", split_axis=1, concat_axis=0, tiled=True)
    grad_kern_weight = fast_einsum("ne,ncp->ecp", all_codes, local_grad)
    grad_kern_bias = jnp.sum(local_grad, axis=0, dtype=jnp.float32)
    code_part = fast_einsum("ncp,ecp->ne", local_grad, kern_low)
    grad_attn_in, grad_attn_out, grad_mlp_in, grad_mlp_out = (
        lax.psum_scatter(grad_in, "dp", scatter_dimension=1, tiled=True),
        lax.psum_scatter(grad_proj, "dp", scatter_dimension=0, tiled=True),
        lax.psum_scatter(grad_up, "dp", scatter_dimension=0, tiled=True),
        lax.psum_scatter(grad_down, "dp", scatter_dimension=0, tiled=True),
    )
    norms_gain = jnp.stack([gain_first, gain_second])
    norms_shift = jnp.stack([shift_first, shift_second])
    code_grad = lax.psum_scatter(code_part, "dp", scatter_dimension=0, tiled=True).reshape(
        slot_count, band_total, hyper_width
    )
    local_hyper = hyper_back((code_grad, patch_bias_grad))
    summed = lax.psum(
        (
            local_hyper[0],
            local_hyper[1],
            local_hyper[2],
            local_hyper[3],
            local_hyper[4],
            local_hyper[5],
            local_hyper[6],
            norms_gain,
            norms_shift,
            grad_in_bias,
            grad_attn_out_bias,
            grad_mlp_in_bias,
            grad_mlp_out_bias,
        ),
        "dp",
    )
    hyper_grads = summed[:7]
    others = summed[7:]
    return (
        layer_out,
        pixel_grad,
        hyper_grads[0],
        hyper_grads[1],
        hyper_grads[2],
        hyper_grads[3],
        hyper_grads[4],
        hyper_grads[5],
        grad_kern_weight,
        grad_kern_bias,
        hyper_grads[6],
        others[0],
        others[1],
        grad_attn_in,
        others[2],
        grad_attn_out,
        others[3],
        grad_mlp_in,
        others[4],
        grad_mlp_out,
        others[5],
    )


def solution(mesh):
    return jax.shard_map(
        per_device,
        mesh=mesh,
        in_specs=(
            P("dp", None, None, None),
            P("dp"),
            P("dp", None),
            P("dp"),
            P("dp", None),
            P(),
            P(),
            P(),
            P(),
            P(),
            P(),
            P(None, "dp", None),
            P("dp", None),
            P(),
            P(),
            P(),
            P(None, "dp", "mp"),
            P(None, "mp"),
            P("dp", "mp"),
            P(),
            P("dp", "mp"),
            P("mp"),
            P("dp", "mp"),
            P(),
            P("dp", None, None),
        ),
        out_specs=(
            P("dp", None, None),
            P("dp", None, None, None),
            P(),
            P(),
            P(),
            P(),
            P(),
            P(),
            P(None, "dp", None),
            P("dp", None),
            P(),
            P(),
            P(),
            P(None, "dp", "mp"),
            P(None, "mp"),
            P("dp", "mp"),
            P(),
            P("dp", "mp"),
            P("mp"),
            P("dp", "mp"),
            P(),
        ),
        check_vma=False,
    )
```

profile of v0, /device:TPU:0, one launch (start us, length us, event | category | flops | bytes accessed | tf_op | source)
XLA Modules:
  0.0 1387.8 jit_solution(8111671895934261146)
XLA Ops:
  9.7 1.6 fusion.136
  18.4 42.9 %all-gather = bf16[1,208,128]{2,0,1:T(2,128)(2,1)S(1)} all-gather(bf16[1,13,128]{2,0,1:T(2,128)(2,1)S(1)} %copy.152), channel_id=2, replica_groups=mesh['dp'=16,'mp'=2] {'dp'}, dimensions={1}, use_global_device_ids=true | all-gather | bytes 56576 | tf_op jit(solution)/shard_map/all_gather | solution.py:146
  61.4 3.2 convert_element_type.166
  64.6 1.7 copy-done.4
  66.2 1.5 add_convert_fusion
  67.8 4.1 copy.154
  72.0 4.7 all-to-all-start
  79.9 134.4 %all_gather.21 = bf16[768,384]{1,0:T(8,128)(2,1)} all-gather(bf16[48,384]{1,0:T(8,128)(2,1)S(1)} %convert_element_type.177), channel_id=1, replica_groups=mesh['dp'=16,'mp'=2] {'dp'}, dimensions={0}, use_global_device_ids=true | all-gather | bytes 626688 | tf_op jit(solution)/shard_map/all_gather | solution.py:162
  214.3 3.1 copy.155
  217.4 1.6 fusion.142
  220.5 2.3 fusion.29
  226.9 1.3 fusion.144
  230.3 32.6 %all-reduce.21.cloned.1.call-done = f32[256,768]{1,0:T(8,128)} async-done(((f32[256,768]{1,0:T(8,128)}), f32[256,768]{1,0:T(8,128)}) %all-reduce.21.cloned.1.call-update) | async-done | bytes 786448 | tf_op jit(solution)/shard_map/psum | solution.py:196
  262.9 1.6 fusion.134
  266.4 63.8 %all-gather.7.cloned.1.call-done = bf16[768,1536]{1,0:T(8,128)(2,1)} async-done(((bf16[48,1536]{1,0:T(8,128)(2,1)}), bf16[768,1536]{1,0:T(8,128)(2,1)}) %all-gather.7.cloned.1.call-update) | async-done | bytes 2359312 | tf_op jit(solution)/shard_map/all_gather | solution.py:163
  330.2 7.1 multiply_convert_fusion.1
  337.2 57.7 %all-gather.9.cloned.1.call-done = bf16[768,1536]{1,0:T(8,128)(2,1)} async-done(((bf16[48,1536]{1,0:T(8,128)(2,1)}), bf16[768,1536]{1,0:T(8,128)(2,1)}) %all-gather.9.cloned.1.call-update) | async-done | bytes 2359312 | tf_op jit(solution)/shard_map/all_gather | solution.py:164
  394.9 4.6 convert_reduce_fusion.1
  400.5 1.7 fusion.145
  402.2 1.3 log_add_fusion
  403.6 3.5 convolution_convert_fusion.1
  407.3 13.1 all-reduce.25.cloned.1.call-done
  420.4 2.0 multiply_reduce_fusion.1
  423.7 19.2 %all-reduce.23.cloned.1.call-done = bf16[256,768]{1,0:T(8,128)(2,1)} async-done(((bf16[256,768]{1,0:T(8,128)(2,1)}), bf16[256,768]{1,0:T(8,128)(2,1)}) %all-reduce.23.cloned.1.call-update) | async-done | bytes 393232 | tf_op jit(solution)/shard_map/psum | solution.py:204
  442.8 2.5 fusion.132
  448.9 1.7 copy.160
  450.7 2.3 convolution_convert_fusion.2
  453.0 1.5 multiply_reduce_fusion
  457.5 3.2 convolution_bitcast_fusion.1
  460.8 20.5 %all-reduce.27.cloned.1.call-done = f32[256,768]{1,0:T(8,128)} async-done(((f32[256,768]{1,0:T(8,128)}), f32[256,768]{1,0:T(8,128)}) %all-reduce.27.cloned.1.call-update) | async-done | bytes 786448 | tf_op jit(solution)/shard_map/psum | solution.py:255
  481.4 2.1 multiply_reduce_fusion.2
  486.9 4.2 convert_bitcast_fusion
  491.0 8.6 copy.169
  499.6 6.8 all-to-all-start.1
  506.8 1.3 fusion.138
  511.2 3.7 convolution_bitcast_fusion
  514.9 6.3 copy.180
  522.0 104.5 %all-to-all-done.1 = bf16[13,768,256]{2,0,1:T(8,128)(2,1)} async-done(((bf16[13,768,256]{2,0,1:T(8,128)(2,1)}), bf16[13,768,256]{2,0,1:T(8,128)(2,1)}, u32[]{:S(2)}, u32[]{:S(2)}) %all-to-all-start.1) | async-done | bytes 5111840 | tf_op jit(solution)/shard_map/all_to_all | solution.py:269
  626.6 5.2 copy.171
  631.8 2.3 copy-done.1
  634.1 4.4 fusion.32
  638.5 61.0 %fusion = f32[16,128]{1,0:T(8,128)S(1)} fusion(f32[208,128]{1,0:T(8,128)S(1)} %fusion.32), kind=kCustom, calls=%all-reduce-scatter | all-reduce-scatter fusion | flops 32769 | bytes 115200
  699.5 1.3 collective-permute-start.1
  700.8 3.6 collective-permute-start
  704.4 1.8 collective-permute-start.2
  708.5 2.4 multiply_add_fusion
  711.0 1.5 fusion.73
  714.5 2.1 fusion.97
  716.6 3.0 fusion.67
  722.5 1.4 fusion.146
  725.1 3.1 fusion.125
  729.6 3.1 fusion.49
  733.8 4.2 fusion.18
  738.0 2.5 copy.181
  740.6 4.6 fusion.1
  745.2 6.3 copy.182
  751.5 4.8 copy.170
  756.5 1.5 convert_reduce_fusion
  758.7 79.2 %all-reduce.13 = (f32[2,128]{1,0:T(2,128)}, f32[2,128]{1,0:T(2,128)}, f32[128]{0:T(128)}, f32[2,768]{1,0:T(2,128)}, f32[2,768]{1,0:T(2,128)}, /*index=5*/f32[2,3...) all-reduce(f32[2,128]{1,0:T(2,128)S(1)} %pad_add_fusion.3, ...), channel_id=1, replica_groups=mesh['dp'=16,'mp'=2] {'dp'}, use_global_device_ids=true, to_apply=%region_33.34 | all-reduce | flops 7552 | bytes 60416 | tf_op jit(solution)/shard_map/psum | solution.py:285
  838.0 125.9 %all-reduce.29.cloned.1.call-done = (f32[4,128,128]{2,1,0:T(8,128)}, f32[128,2048]{1,0:T(8,128)}, f32[2048,128]{1,0:T(8,128)}, f32[128,768]{1,0:T(8,128)}, f32[3,768,384]{2,0,1:T(4,128)}) async-done(((f32[4,128,128]{2,1,0:T(8,128)}, f32[128,2048]{1,0:T(8,128)}, f32[2048,128]{1,0:T(8,128)}, f32[128,768]{1,0:T(8,128)}, f32[3,768,384]{2,0,1:T(4,128)}), (f32[4,128,128]{2,1,0:T(8,128)}, f32[128,2048]{1,0:T(8,128)}, ...) | async-done | bytes 6291472 | tf_op jit(solution)/shard_map/psum | solution.py:285
  965.7 126.9 %reduce-scatter.6.cloned.1.call-done = f32[48,384]{1,0:T(8,128)} async-done(((f32[768,384]{1,0:T(8,128)}), f32[48,384]{1,0:T(8,128)}) %reduce-scatter.6.cloned.1.call-update) | async-done | bytes 73744 | tf_op jit(solution)/shard_map/reduce_scatter | solution.py:275
  1092.6 142.0 %reduce-scatter.8.cloned.1.call-done = f32[48,1536]{1,0:T(8,128)} async-done(((f32[768,1536]{1,0:T(8,128)}), f32[48,1536]{1,0:T(8,128)}) %reduce-scatter.8.cloned.1.call-update) | async-done | bytes 294928 | tf_op jit(solution)/shard_map/reduce_scatter | solution.py:276
  1234.6 141.9 %reduce-scatter.10.cloned.1.call-done = f32[48,1536]{1,0:T(8,128)} async-done(((f32[768,1536]{1,0:T(8,128)}), f32[48,1536]{1,0:T(8,128)}) %reduce-scatter.10.cloned.1.call-update) | async-done | bytes 294928 | tf_op jit(solution)/shard_map/reduce_scatter | solution.py:277
  1376.4 1.7 copy.226
  (407 shorter events, 51.9 us)
Async XLA Ops:
  7.2 8.6 copy-start
  7.2 6.7 copy-start.110
  7.2 8.5 copy-start.114
  7.2 8.5 copy-start.115
  7.2 9.2 copy-start.126
  11.8 5.7 copy-start.51
  12.2 5.3 copy-start.47
  12.6 4.9 copy-start.49
  12.9 4.6 copy-start.73
  17.8 46.8 %copy-start.123 = (f32[14]{0:T(128)}, f32[14]{0:T(128)S(1)}, u32[]{:S(2)}) copy-start(f32[14]{0:T(128)S(1)} %multiply_reduce_fusion.8) | copy-start | bytes 172
  18.3 61.1 %copy-start.62 = (f32[1,14,128]{2,1,0:T(8,128)}, f32[1,14,128]{2,1,0:T(8,128)S(1)}, u32[]{:S(2)}) copy-start(f32[1,14,128]{2,1,0:T(8,128)S(1)} %add_bitcast_fusion) | copy-start | bytes 21508
  61.4 4.9 copy-start.63
  71.9 4.8 copy-start.44
  71.9 6.2 copy-start.59
  71.9 6.9 copy-start.113
  71.9 7.4 copy-start.101
  71.9 7.4 copy-start.102
  71.9 7.5 copy-start.28
  72.0 7.8 copy-start.107
  72.0 142.3 %all-to-all-start = ((bf16[208,48,256]{2,1,0:T(8,128)(2,1)}), bf16[208,48,256]{2,1,0:T(8,128)(2,1)}, u32[]{:S(2)}, u32[]{:S(2)}) async-start(bf16[208,48,256]{2,1,0:T(8,128)(2,1)} %copy.154), calls=%async_computation | async-start | bytes 10223616 | tf_op jit(solution)/shard_map/all_to_all | solution.py:149
  76.7 143.2 %all-gather.5.cloned.1.call-start = ((), (), s32[]{:S(2)}) async-start(), calls=%async_computation.5 | async-start | bytes 1880064 | tf_op jit(solution)/shard_map/all_gather | solution.py:161
  77.5 185.5 %all-reduce.21.cloned.1.call-start = ((), (), s32[]{:S(2)}) async-start(), calls=%async_computation.6 | async-start | bytes 1572864 | tf_op jit(solution)/shard_map/psum | solution.py:196
  78.8 138.5 %copy-start.118 = (bf16[13]{0:T(256)(128)(2,1)}, bf16[13]{0:T(256)(128)(2,1)S(1)}, u32[]{:S(2)}) copy-start(bf16[13]{0:T(256)(128)(2,1)S(1)} %get-tuple-element.189) | copy-start | bytes 82
  79.4 140.5 %copy-start.60 = (f32[768]{0:T(1024)}, f32[768]{0:T(1024)S(1)}, u32[]{:S(2)}) copy-start(f32[768]{0:T(1024)S(1)} %get-tuple-element.192) | copy-start | bytes 9220
  79.4 140.5 %copy-start.77 = (f32[768]{0:T(1024)}, f32[768]{0:T(1024)S(1)}, u32[]{:S(2)}) copy-start(f32[768]{0:T(1024)S(1)} %get-tuple-element.120) | copy-start | bytes 9220
  228.2 102.0 %all-gather.7.cloned.1.call-start = ((), (), s32[]{:S(2)}) async-start(), calls=%async_computation.7 | async-start | bytes 2506752 | tf_op jit(solution)/shard_map/all_gather | solution.py:163
  228.9 166.0 %all-gather.9.cloned.1.call-start = ((), (), s32[]{:S(2)}) async-start(), calls=%async_computation.8 | async-start | bytes 2506752 | tf_op jit(solution)/shard_map/all_gather | solution.py:164
  229.7 190.7 %all-reduce.25.cloned.1.call-start = ((), (), s32[]{:S(2)}) async-start(), calls=%async_computation.10 | async-start | bytes 1572864 | tf_op jit(solution)/shard_map/psum | solution.py:222
  394.9 5.5 copy-start.125
  402.2 40.6 %all-reduce.23.cloned.1.call-start = ((), (), s32[]{:S(2)}) async-start(), calls=%async_computation.9 | async-start | bytes 786432 | tf_op jit(solution)/shard_map/psum | solution.py:204
  403.6 16.8 %copy-start.65 = (f32[256]{0:T(256)S(1)}, f32[256]{0:T(256)}, u32[]{:S(2)}) copy-start(f32[256]{0:T(256)} %copy-done.64) | copy-start | bytes 3076
  407.0 35.8 %copy-start.67 = (f32[256]{0:T(256)S(1)}, f32[256]{0:T(256)}, u32[]{:S(2)}) copy-start(f32[256]{0:T(256)} %compare_convert_fusion) | copy-start | bytes 3076
  407.1 74.3 %all-reduce.27.cloned.1.call-start = ((), (), s32[]{:S(2)}) async-start(), calls=%async_computation.11 | async-start | bytes 1572864 | tf_op jit(solution)/shard_map/psum | solution.py:255
  447.1 5.9 copy-start.54
  456.5 4.3 copy-start.33
  457.5 23.8 %copy-start.3 = (f32[256,768]{1,0:T(8,128)S(1)}, f32[256,768]{1,0:T(8,128)}, u32[]{:S(2)}) copy-start(f32[256,768]{1,0:T(8,128)} %copy-done.2) | copy-start | bytes 2359300
  457.5 23.8 %copy-start.61 = (f32[768]{0:T(1024)S(1)}, f32[768]{0:T(1024)}, u32[]{:S(2)}) copy-start(f32[768]{0:T(1024)} %copy-done.60) | copy-start | bytes 9220
  457.5 23.8 %copy-start.72 = (f32[256]{0:T(256)S(1)}, f32[256]{0:T(256)}, u32[]{:S(2)}) copy-start(f32[256]{0:T(256)} %copy-done.71) | copy-start | bytes 3076
  499.6 126.9 %all-to-all-start.1 = ((bf16[13,768,256]{2,0,1:T(8,128)(2,1)}), bf16[13,768,256]{2,0,1:T(8,128)(2,1)}, u32[]{:S(2)}, u32[]{:S(2)}) async-start(bf16[13,768,256]{2,0,1:T(8,128)(2,1)} %copy.169), calls=%async_computation.1 | async-start | bytes 12582912 | tf_op jit(solution)/shard_map/all_to_all | solution.py:269
  506.5 457.4 %all-reduce.29.cloned.1.call-start = ((), (), s32[]{:S(2)}) async-start(), calls=%async_computation.15 | async-start | bytes 14942208 | tf_op jit(solution)/shard_map/psum | solution.py:285
  514.9 6.3 copy-start.120
  626.6 7.5 copy-start.5
  634.1 72.1 %copy-start.29 = (f32[128,768]{1,0:T(8,128)S(1)}, f32[128,768]{1,0:T(8,128)}, u32[]{:S(2)}) copy-start(f32[128,768]{1,0:T(8,128)} %param.38) | copy-start | bytes 1179652
  634.1 73.4 %copy-start.95 = (f32[14]{0:T(128)S(1)}, f32[14]{0:T(128)}, u32[]{:S(2)}) copy-start(f32[14]{0:T(128)} %copy-done.94) | copy-start | bytes 172
  634.1 73.4 %copy-start.97 = (f32[128]{0:T(128)S(1)}, f32[128]{0:T(128)}, u32[]{:S(2)}) copy-start(f32[128]{0:T(128)} %copy-done.96) | copy-start | bytes 1540
  634.1 73.4 %copy-start.106 = (f32[14]{0:T(128)S(1)}, f32[14]{0:T(128)}, u32[]{:S(2)}) copy-start(f32[14]{0:T(128)} %copy-done.105) | copy-start | bytes 172
  634.1 74.1 %copy-start.124 = (f32[14]{0:T(128)S(1)}, f32[14]{0:T(128)}, u32[]{:S(2)}) copy-start(f32[14]{0:T(128)} %copy-done.123) | copy-start | bytes 172
  634.1 74.3 %copy-start.46 = (f32[14,2048]{1,0:T(8,128)S(1)}, f32[14,2048]{1,0:T(8,128)}, u32[]{:S(2)}) copy-start(f32[14,2048]{1,0:T(8,128)} %copy-done.45) | copy-start | bytes 344068
  699.5 7.6 collective-permute-start.1
  700.8 6.3 collective-permute-start
  704.4 2.6 collective-permute-start.2
  708.5 4.3 copy-start.43
  708.5 4.7 copy-start.42
  708.5 4.7 copy-start.52
  708.5 4.7 copy-start.74
  708.5 4.7 copy-start.93
  708.5 4.9 copy-start.50
  708.5 4.9 copy-start.99
  708.5 4.9 copy-start.117
  721.5 371.1 %reduce-scatter.6.cloned.1.call-start = ((), (), s32[]{:S(2)}) async-start(), calls=%async_computation.12 | async-start | bytes 1253376 | tf_op jit(solution)/shard_map/reduce_scatter | solution.py:275
  724.0 510.6 %reduce-scatter.8.cloned.1.call-start = ((), (), s32[]{:S(2)}) async-start(), calls=%async_computation.13 | async-start | bytes 5013504 | tf_op jit(solution)/shard_map/reduce_scatter | solution.py:276
  728.2 648.2 %reduce-scatter.10.cloned.1.call-start = ((), (), s32[]{:S(2)}) async-start(), calls=%async_computation.14 | async-start | bytes 5013504 | tf_op jit(solution)/shard_map/reduce_scatter | solution.py:277
  963.9 414.2 %copy-start.32 = (f32[128,2048]{1,0:T(8,128)S(1)}, f32[128,2048]{1,0:T(8,128)}, u32[]{:S(2)}) copy-start(f32[128,2048]{1,0:T(8,128)} %get-tuple-element.197) | copy-start | bytes 3145732
  965.0 414.1 %copy-start.31 = (f32[2048,128]{1,0:T(8,128)S(1)}, f32[2048,128]{1,0:T(8,128)}, u32[]{:S(2)}) copy-start(f32[2048,128]{1,0:T(8,128)} %get-tuple-element.198) | copy-start | bytes 3145732
  (80 other events, 143.4 us)
Sparse Core Ops, SparseCore 0:
  80.8 105.2 all-gather.4
  228.3 34.5 all-reduce.20
  266.7 63.4 all-gather.6
  333.8 61.0 all-gather.8
  402.3 18.0 all-reduce.24
  423.1 19.6 all-reduce.22
  460.9 20.3 all-reduce.26
  721.6 242.2 all-reduce.28
  969.9 122.6 reduce-scatter.5
  1099.0 135.5 reduce-scatter.7
  1240.3 136.0 reduce-scatter.9
where the time goes:
time: 1400 us; the launch traced here: 1390 us
  waiting for transfers between devices  849 us (61%)
  blocking collectives  318 us (23%)
  matrix products  79.3 us (6%)
  local copies, waits for them, and re-layouts  73.6 us (5%)
  other arithmetic  30.8 us (2%)
  starting transfers between devices  19.3 us (1%)
  between operations  18.5 us (1%)
    reduce_scatter x1, waiting for transfers between devices, per_device(): lax.psum_scatter(grad_up, 'dp', scatter_dimension=0, tiled=True)  142 us
    reduce_scatter x1, waiting for transfers between devices, per_device(): lax.psum_scatter(grad_down, 'dp', scatter_dimension=0, tiled=True)  142 us
    all_gather x1, blocking collectives, per_device(): lax.all_gather(weight_shards[1], 'dp', axis=0, tiled=True)  134 us
    reduce_scatter x1, waiting for transfers between devices, per_device(): lax.psum_scatter(grad_proj, 'dp', scatter_dimension=0, tiled=True)  127 us
    psum x1, waiting for transfers between devices, per_device(): lax.psum((local_hyper[0], local_hyper[1], local_hyper[2], local_hyper[3],...  126 us
    all_to_all x1, waiting for transfers between devices, per_device(): lax.all_to_all(kernel_grad, 'dp', split_axis=1, concat_axis=0, tiled=True)  105 us
    psum x1, blocking collectives, per_device(): lax.psum((local_hyper[0], local_hyper[1], local_hyper[2], local_hyper[3],...  79.2 us
    all_gather x1, waiting for transfers between devices, per_device(): lax.all_gather(weight_shards[2], 'dp', axis=0, tiled=True)  63.8 us
  transfers between devices with their start and end apart: 16, of which 12 were waited for; matrix products, arithmetic and copies ran while one was open for 5% of the time, Pallas kernels for 0%

commit v1 on v0

--- a/solution.py
+++ b/solution.py
@@ -266,7 +266,10 @@
         .astype(jnp.bfloat16)
         .reshape(slot_count * band_total, model_width, pix_size)
     )
-    local_grad = lax.all_to_all(kernel_grad, "dp", split_axis=1, concat_axis=0, tiled=True)
+    local_grad = jnp.concatenate(
+        lax.all_to_all(jnp.stack(jnp.split(kernel_grad, lax.axis_size("dp"), axis=1)), "dp", 0, 0),
+        axis=0,
+    )
     grad_kern_weight = fast_einsum("ne,ncp->ecp", all_codes, local_grad)
     grad_kern_bias = jnp.sum(local_grad, axis=0, dtype=jnp.float32)
     code_part = fast_einsum("ncp,ecp->ne", local_grad, kern_low)

time: 1400 us -> 1410 us (level)
  local copies, waits for them, and re-layouts: 73.6 us -> 110 us
  waiting for transfers between devices: 849 us -> 829 us
    another operation x5 -> x23, local copies, waits for them, and re-layouts: 1.5 us -> 44 us  [the longest x18 42.5 us: per_device(): jnp.stack(jnp.split(kernel_grad, lax.axis_size('dp'), axis=1))]
    all_to_all x1, waiting for transfers between devices: 105 us -> 82.2 us  [per_device(): lax.all_to_all(jnp.stack(jnp.split(kernel_grad, lax.axis_size('dp'), axis...]
    unnamed x267 -> x304, local copies, waits for them, and re-layouts: 34.5 us -> 46.7 us
where the time goes in v1:
time: 1410 us; the launch traced here: 1400 us
  waiting for transfers between devices  829 us (59%)
  blocking collectives  313 us (22%)
  local copies, waits for them, and re-layouts  110 us (8%)
  matrix products  80.3 us (6%)
  other arithmetic  33.2 us (2%)
  between operations  18.5 us (1%)
  starting transfers between devices  18.2 us (1%)
    reduce_scatter x1, waiting for transfers between devices, per_device(): lax.psum_scatter(grad_up, 'dp', scatter_dimension=0, tiled=True)  142 us
    reduce_scatter x1, waiting for transfers between devices, per_device(): lax.psum_scatter(grad_down, 'dp', scatter_dimension=0, tiled=True)  142 us
    all_gather x1, blocking collectives, per_device(): lax.all_gather(weight_shards[1], 'dp', axis=0, tiled=True)  134 us
    psum x1, waiting for transfers between devices, per_device(): lax.psum((local_hyper[0], local_hyper[1], local_hyper[2], local_hyper[3],...  128 us
    reduce_scatter x1, waiting for transfers between devices, per_device(): lax.psum_scatter(grad_proj, 'dp', scatter_dimension=0, tiled=True)  127 us
    all_to_all x1, waiting for transfers between devices, per_device(): lax.all_to_all(jnp.stack(jnp.split(kernel_grad, lax.axis_size('dp'), axis...  82.2 us
    psum x1, blocking collectives, per_device(): lax.psum((local_hyper[0], local_hyper[1], local_hyper[2], local_hyper[3],...  79.4 us
    all_gather x1, waiting for transfers between devices, per_device(): lax.all_gather(weight_shards[2], 'dp', axis=0, tiled=True)  63.8 us
  transfers between devices with their start and end apart: 16, of which 12 were waited for; matrix products, arithmetic and copies ran while one was open for 5% of the time, Pallas kernels for 0%

profile of v1, /device:TPU:0, one launch (start us, length us, event | category | flops | bytes accessed | tf_op | source)
XLA Modules:
  0.0 1402.9 jit_solution(11782755426984809266)
XLA Ops:
  18.6 42.9 %all-gather = bf16[1,208,128]{2,0,1:T(2,128)(2,1)S(1)} all-gather(bf16[1,13,128]{2,0,1:T(2,128)(2,1)S(1)} %copy.165), channel_id=2, replica_groups=mesh['dp'=16,'mp'=2] {'dp'}, dimensions={1}, use_global_device_ids=true | all-gather | bytes 56576 | tf_op jit(solution)/shard_map/all_gather | solution.py:146
  61.5 3.2 convert_element_type.166
  67.9 4.1 copy.167
  72.1 4.7 all-to-all-start
  80.0 134.4 %all_gather.21 = bf16[768,384]{1,0:T(8,128)(2,1)} all-gather(bf16[48,384]{1,0:T(8,128)(2,1)S(1)} %convert_element_type.177), channel_id=1, replica_groups=mesh['dp'=16,'mp'=2] {'dp'}, dimensions={0}, use_global_device_ids=true | all-gather | bytes 626688 | tf_op jit(solution)/shard_map/all_gather | solution.py:162
  214.4 3.1 copy.168
  220.7 2.3 fusion.29
  230.4 32.6 %all-reduce.21.cloned.1.call-done = f32[256,768]{1,0:T(8,128)} async-done(((f32[256,768]{1,0:T(8,128)}), f32[256,768]{1,0:T(8,128)}) %all-reduce.21.cloned.1.call-update) | async-done | bytes 786448 | tf_op jit(solution)/shard_map/psum | solution.py:196
  266.5 63.8 %all-gather.7.cloned.1.call-done = bf16[768,1536]{1,0:T(8,128)(2,1)} async-done(((bf16[48,1536]{1,0:T(8,128)(2,1)}), bf16[768,1536]{1,0:T(8,128)(2,1)}) %all-gather.7.cloned.1.call-update) | async-done | bytes 2359312 | tf_op jit(solution)/shard_map/all_gather | solution.py:163
  330.3 7.0 multiply_convert_fusion.1
  337.3 57.7 %all-gather.9.cloned.1.call-done = bf16[768,1536]{1,0:T(8,128)(2,1)} async-done(((bf16[48,1536]{1,0:T(8,128)(2,1)}), bf16[768,1536]{1,0:T(8,128)(2,1)}) %all-gather.9.cloned.1.call-update) | async-done | bytes 2359312 | tf_op jit(solution)/shard_map/all_gather | solution.py:164
  395.0 4.6 convert_reduce_fusion.1
  403.7 3.5 convolution_convert_fusion.1
  407.4 13.1 all-reduce.25.cloned.1.call-done
  420.5 2.0 multiply_reduce_fusion.1
  423.8 19.2 %all-reduce.23.cloned.1.call-done = bf16[256,768]{1,0:T(8,128)(2,1)} async-done(((bf16[256,768]{1,0:T(8,128)(2,1)}), bf16[256,768]{1,0:T(8,128)(2,1)}) %all-reduce.23.cloned.1.call-update) | async-done | bytes 393232 | tf_op jit(solution)/shard_map/psum | solution.py:204
  443.0 2.5 fusion.132
  450.8 2.3 convolution_convert_fusion.2
  457.6 3.2 convolution_bitcast_fusion.1
  460.9 20.5 %all-reduce.27.cloned.1.call-done = f32[256,768]{1,0:T(8,128)} async-done(((f32[256,768]{1,0:T(8,128)}), f32[256,768]{1,0:T(8,128)}) %all-reduce.27.cloned.1.call-update) | async-done | bytes 786448 | tf_op jit(solution)/shard_map/psum | solution.py:255
  481.4 2.1 multiply_reduce_fusion.2
  486.9 1.9 convert_bitcast_fusion
  488.8 7.1 slice_bitcast_fusion
  495.9 2.2 copy.197
  498.0 2.2 copy.196
  500.2 2.2 copy.195
  502.4 2.2 copy.194
  504.6 2.2 copy.193
  506.8 2.2 copy.192
  508.9 2.2 copy.191
  511.1 2.2 copy.190
  513.3 2.2 copy.189
  515.4 2.1 copy.188
  517.6 2.2 copy.187
  519.8 2.2 copy.186
  521.9 2.2 copy.185
  524.1 2.2 copy.184
  526.3 2.2 copy.183
  528.4 2.2 copy.182
  530.6 1.8 constant_dynamic-update-slice_fusion.15
  532.4 1.8 constant_dynamic-update-slice_fusion.14
  534.2 1.8 constant_dynamic-update-slice_fusion.13
  545.8 6.8 all-to-all-start.1
  557.2 3.7 convolution_bitcast_fusion
  560.9 6.7 copy.207
  568.5 82.2 %all-to-all-done.1 = bf16[16,13,48,256]{3,2,1,0:T(8,128)(2,1)} async-done(((bf16[16,13,48,256]{3,2,1,0:T(8,128)(2,1)}), bf16[16,13,48,256]{3,2,1,0:T(8,128)(2,1)}, u32[]{:S(2)}, u32[]{:S(2)}) %all-to-all-start.1) | async-done | bytes 5111840 | tf_op jit(solution)/shard_map/all_to_all | solution.py:270
  650.7 7.8 fusion.32
  658.5 56.5 %fusion = f32[16,128]{1,0:T(8,128)S(1)} fusion(f32[208,128]{1,0:T(8,128)S(1)} %fusion.32), kind=kCustom, calls=%all-reduce-scatter | all-reduce-scatter fusion | flops 32769 | bytes 115200
  716.3 3.2 collective-permute-start
  723.7 2.4 multiply_add_fusion
  729.6 2.1 fusion.97
  731.7 3.0 fusion.67
  740.3 3.1 fusion.125
  744.7 3.0 fusion.49
  748.8 4.2 fusion.18
  753.0 2.5 copy.208
  755.6 4.6 fusion.1
  760.2 6.3 copy.209
  766.6 4.0 convert_reduce_fusion
  771.4 79.4 %all-reduce.13 = (f32[2,128]{1,0:T(2,128)}, f32[2,128]{1,0:T(2,128)}, f32[128]{0:T(128)}, f32[2,768]{1,0:T(2,128)}, f32[2,768]{1,0:T(2,128)}, /*index=5*/f32[2,3...) all-reduce(f32[2,128]{1,0:T(2,128)S(1)} %pad_add_fusion.3, ...), channel_id=1, replica_groups=mesh['dp'=16,'mp'=2] {'dp'}, use_global_device_ids=true, to_apply=%region_33.34 | all-reduce | flops 7552 | bytes 60416 | tf_op jit(solution)/shard_map/psum | solution.py:288
  850.8 128.2 %all-reduce.29.cloned.1.call-done = (f32[4,128,128]{2,1,0:T(8,128)}, f32[128,2048]{1,0:T(8,128)}, f32[2048,128]{1,0:T(8,128)}, f32[128,768]{1,0:T(8,128)}, f32[3,768,384]{2,0,1:T(4,128)}) async-done(((f32[4,128,128]{2,1,0:T(8,128)}, f32[128,2048]{1,0:T(8,128)}, f32[2048,128]{1,0:T(8,128)}, f32[128,768]{1,0:T(8,128)}, f32[3,768,384]{2,0,1:T(4,128)}), (f32[4,128,128]{2,1,0:T(8,128)}, f32[128,2048]{1,0:T(8,128)}, ...) | async-done | bytes 6291472 | tf_op jit(solution)/shard_map/psum | solution.py:288
  980.8 126.9 %reduce-scatter.6.cloned.1.call-done = f32[48,384]{1,0:T(8,128)} async-done(((f32[768,384]{1,0:T(8,128)}), f32[48,384]{1,0:T(8,128)}) %reduce-scatter.6.cloned.1.call-update) | async-done | bytes 73744 | tf_op jit(solution)/shard_map/reduce_scatter | solution.py:278
  1107.7 142.0 %reduce-scatter.8.cloned.1.call-done = f32[48,1536]{1,0:T(8,128)} async-done(((f32[768,1536]{1,0:T(8,128)}), f32[48,1536]{1,0:T(8,128)}) %reduce-scatter.8.cloned.1.call-update) | async-done | bytes 294928 | tf_op jit(solution)/shard_map/reduce_scatter | solution.py:279
  1249.7 141.9 %reduce-scatter.10.cloned.1.call-done = f32[48,1536]{1,0:T(8,128)} async-done(((f32[768,1536]{1,0:T(8,128)}), f32[48,1536]{1,0:T(8,128)}) %reduce-scatter.10.cloned.1.call-update) | async-done | bytes 294928 | tf_op jit(solution)/shard_map/reduce_scatter | solution.py:280
  (459 shorter events, 85.9 us)
Async XLA Ops:
  7.2 8.7 copy-start
  7.2 6.7 copy-start.121
  7.2 8.6 copy-start.125
  7.2 8.6 copy-start.126
  7.2 9.3 copy-start.137
  11.8 5.8 copy-start.62
  12.2 5.4 copy-start.58
  12.6 4.9 copy-start.60
  17.9 46.8 %copy-start.134 = (f32[14]{0:T(128)}, f32[14]{0:T(128)S(1)}, u32[]{:S(2)}) copy-start(f32[14]{0:T(128)S(1)} %multiply_reduce_fusion.8) | copy-start | bytes 172
  18.5 61.0 %copy-start.73 = (f32[1,14,128]{2,1,0:T(8,128)}, f32[1,14,128]{2,1,0:T(8,128)S(1)}, u32[]{:S(2)}) copy-start(f32[1,14,128]{2,1,0:T(8,128)S(1)} %add_bitcast_fusion) | copy-start | bytes 21508
  61.5 4.9 copy-start.74
  72.1 4.8 copy-start.55
  72.1 6.2 copy-start.70
  72.1 6.9 copy-start.124
  72.1 7.4 copy-start.112
  72.1 7.4 copy-start.113
  72.1 7.4 copy-start.26
  72.1 7.8 copy-start.118
  72.1 142.3 %all-to-all-start = ((bf16[208,48,256]{2,1,0:T(8,128)(2,1)}), bf16[208,48,256]{2,1,0:T(8,128)(2,1)}, u32[]{:S(2)}, u32[]{:S(2)}) async-start(bf16[208,48,256]{2,1,0:T(8,128)(2,1)} %copy.167), calls=%async_computation | async-start | bytes 10223616 | tf_op jit(solution)/shard_map/all_to_all | solution.py:149
  76.9 143.2 %all-gather.5.cloned.1.call-start = ((), (), s32[]{:S(2)}) async-start(), calls=%async_computation.5 | async-start | bytes 1880064 | tf_op jit(solution)/shard_map/all_gather | solution.py:161
  77.6 185.4 %all-reduce.21.cloned.1.call-start = ((), (), s32[]{:S(2)}) async-start(), calls=%async_computation.6 | async-start | bytes 1572864 | tf_op jit(solution)/shard_map/psum | solution.py:196
  78.9 138.6 %copy-start.129 = (bf16[13]{0:T(256)(128)(2,1)}, bf16[13]{0:T(256)(128)(2,1)S(1)}, u32[]{:S(2)}) copy-start(bf16[13]{0:T(256)(128)(2,1)S(1)} %get-tuple-element.205) | copy-start | bytes 82
  79.5 140.6 %copy-start.71 = (f32[768]{0:T(1024)}, f32[768]{0:T(1024)S(1)}, u32[]{:S(2)}) copy-start(f32[768]{0:T(1024)S(1)} %get-tuple-element.208) | copy-start | bytes 9220
  79.5 140.6 %copy-start.88 = (f32[768]{0:T(1024)}, f32[768]{0:T(1024)S(1)}, u32[]{:S(2)}) copy-start(f32[768]{0:T(1024)S(1)} %get-tuple-element.120) | copy-start | bytes 9220
  228.3 102.0 %all-gather.7.cloned.1.call-start = ((), (), s32[]{:S(2)}) async-start(), calls=%async_computation.7 | async-start | bytes 2506752 | tf_op jit(solution)/shard_map/all_gather | solution.py:163
  229.0 166.0 %all-gather.9.cloned.1.call-start = ((), (), s32[]{:S(2)}) async-start(), calls=%async_computation.8 | async-start | bytes 2506752 | tf_op jit(solution)/shard_map/all_gather | solution.py:164
  229.8 190.7 %all-reduce.25.cloned.1.call-start = ((), (), s32[]{:S(2)}) async-start(), calls=%async_computation.10 | async-start | bytes 1572864 | tf_op jit(solution)/shard_map/psum | solution.py:222
  395.0 5.6 copy-start.136
  402.3 40.6 %all-reduce.23.cloned.1.call-start = ((), (), s32[]{:S(2)}) async-start(), calls=%async_computation.9 | async-start | bytes 786432 | tf_op jit(solution)/shard_map/psum | solution.py:204
  403.7 16.8 %copy-start.76 = (f32[256]{0:T(256)S(1)}, f32[256]{0:T(256)}, u32[]{:S(2)}) copy-start(f32[256]{0:T(256)} %copy-done.75) | copy-start | bytes 3076
  407.1 35.8 %copy-start.78 = (f32[256]{0:T(256)S(1)}, f32[256]{0:T(256)}, u32[]{:S(2)}) copy-start(f32[256]{0:T(256)} %compare_convert_fusion) | copy-start | bytes 3076
  407.2 74.2 %all-reduce.27.cloned.1.call-start = ((), (), s32[]{:S(2)}) async-start(), calls=%async_computation.11 | async-start | bytes 1572864 | tf_op jit(solution)/shard_map/psum | solution.py:255
  447.2 5.8 copy-start.65
  457.6 23.8 %copy-start.2 = (f32[256,768]{1,0:T(8,128)S(1)}, f32[256,768]{1,0:T(8,128)}, u32[]{:S(2)}) copy-start(f32[256,768]{1,0:T(8,128)} %copy-done.1) | copy-start | bytes 2359300
  457.6 23.8 %copy-start.72 = (f32[768]{0:T(1024)S(1)}, f32[768]{0:T(1024)}, u32[]{:S(2)}) copy-start(f32[768]{0:T(1024)} %copy-done.71) | copy-start | bytes 9220
  457.6 23.8 %copy-start.83 = (f32[256]{0:T(256)S(1)}, f32[256]{0:T(256)}, u32[]{:S(2)}) copy-start(f32[256]{0:T(256)} %copy-done.82) | copy-start | bytes 3076
  530.6 5.4 copy-start.40
  530.6 6.1 copy-start.39
  530.6 6.9 copy-start.38
  532.4 5.8 copy-start.37
  534.2 4.8 copy-start.36
  545.8 104.8 %all-to-all-start.1 = ((bf16[16,13,48,256]{3,2,1,0:T(8,128)(2,1)}), bf16[16,13,48,256]{3,2,1,0:T(8,128)(2,1)}, u32[]{:S(2)}, u32[]{:S(2)}) async-start(bf16[16,13,48,256]{3,2,1,0:T(8,128)(2,1)} %constant_dynamic-update-slice_fusion), calls=%async_computation.1 | async-start | bytes 10223616 | tf_op jit(solution)/shard_map/all_to_all | solution.py:270
  552.7 426.3 %all-reduce.29.cloned.1.call-start = ((), (), s32[]{:S(2)}) async-start(), calls=%async_computation.15 | async-start | bytes 14942208 | tf_op jit(solution)/shard_map/psum | solution.py:288
  560.9 6.8 copy-start.131
  650.6 70.2 %copy-start.27 = (f32[128,768]{1,0:T(8,128)S(1)}, f32[128,768]{1,0:T(8,128)}, u32[]{:S(2)}) copy-start(f32[128,768]{1,0:T(8,128)} %param.38) | copy-start | bytes 1179652
  650.6 71.9 %copy-start.106 = (f32[14]{0:T(128)S(1)}, f32[14]{0:T(128)}, u32[]{:S(2)}) copy-start(f32[14]{0:T(128)} %copy-done.105) | copy-start | bytes 172
  650.6 71.9 %copy-start.108 = (f32[128]{0:T(128)S(1)}, f32[128]{0:T(128)}, u32[]{:S(2)}) copy-start(f32[128]{0:T(128)} %copy-done.107) | copy-start | bytes 1540
  650.6 71.9 %copy-start.117 = (f32[14]{0:T(128)S(1)}, f32[14]{0:T(128)}, u32[]{:S(2)}) copy-start(f32[14]{0:T(128)} %copy-done.116) | copy-start | bytes 172
  650.6 72.7 %copy-start.135 = (f32[14]{0:T(128)S(1)}, f32[14]{0:T(128)}, u32[]{:S(2)}) copy-start(f32[14]{0:T(128)} %copy-done.134) | copy-start | bytes 172
  650.7 72.9 %copy-start.57 = (f32[14,2048]{1,0:T(8,128)S(1)}, f32[14,2048]{1,0:T(8,128)}, u32[]{:S(2)}) copy-start(f32[14,2048]{1,0:T(8,128)} %copy-done.56) | copy-start | bytes 344068
  715.0 7.2 collective-permute-start.1
  716.3 5.9 collective-permute-start
  719.5 2.6 collective-permute-start.2
  723.7 4.9 copy-start.61
  723.7 4.9 copy-start.110
  723.7 4.9 copy-start.128
  736.6 371.1 %reduce-scatter.6.cloned.1.call-start = ((), (), s32[]{:S(2)}) async-start(), calls=%async_computation.12 | async-start | bytes 1253376 | tf_op jit(solution)/shard_map/reduce_scatter | solution.py:278
  739.2 510.5 %reduce-scatter.8.cloned.1.call-start = ((), (), s32[]{:S(2)}) async-start(), calls=%async_computation.13 | async-start | bytes 5013504 | tf_op jit(solution)/shard_map/reduce_scatter | solution.py:279
  743.4 648.2 %reduce-scatter.10.cloned.1.call-start = ((), (), s32[]{:S(2)}) async-start(), calls=%async_computation.14 | async-start | bytes 5013504 | tf_op jit(solution)/shard_map/reduce_scatter | solution.py:280
  766.6 4.8 copy-start.86
  766.6 4.8 copy-start.87
  766.6 4.8 copy-start.111
  979.0 414.2 %copy-start.43 = (f32[128,2048]{1,0:T(8,128)S(1)}, f32[128,2048]{1,0:T(8,128)}, u32[]{:S(2)}) copy-start(f32[128,2048]{1,0:T(8,128)} %get-tuple-element.213) | copy-start | bytes 3145732
  980.1 414.1 %copy-start.42 = (f32[2048,128]{1,0:T(8,128)S(1)}, f32[2048,128]{1,0:T(8,128)}, u32[]{:S(2)}) copy-start(f32[2048,128]{1,0:T(8,128)} %get-tuple-element.214) | copy-start | bytes 3145732
  (91 other events, 211.9 us)
Sparse Core Ops, SparseCore 0:
  81.0 105.2 all-gather.4
  228.4 34.5 all-reduce.20
  266.8 63.4 all-gather.6
  333.9 61.0 all-gather.8
  402.4 18.0 all-reduce.24
  423.3 19.6 all-reduce.22
  461.0 20.3 all-reduce.26
  736.7 242.2 all-reduce.28
  985.1 122.6 reduce-scatter.5
  1114.1 135.5 reduce-scatter.7
  1255.5 136.0 reduce-scatter.9
